TPU v7x, 256 devices: a whole 4x4x8 slice. The times are simulated.
256 devices in a mesh: rows: 64 (over x, y, z_hi), sub: 4 (over z_lo, core).
Axes of the slice: x: 4, y: 4, z: 8 (z_hi: 4, z_lo: 2; z = z_hi * 2 + z_lo), core: 2. Of those that a mesh axis runs over, the one named last changes fastest.
Arguments:
- right_sides: float32 [262144, 512], P(('rows', 'sub')), may hold values from -6 to 6
- bases_u: float32 [4, 262144, 256], P(None, ('rows', 'sub')), may hold values from -0.375 to 0.375
- bases_v: float32 [4, 262144, 256], P(None, ('rows', 'sub')), may hold values from -0.015625 to 0.015625
- couple_first: float32 [512, 512], P(('rows', 'sub')), may hold values from -0.25 to 0.25
- couple_second: float32 [1024, 512], P(('rows', 'sub')), may hold values from -0.25 to 0.25
- couple_third: float32 [2048, 512], P(('rows', 'sub')), may hold values from -0.25 to 0.25
- couple_fourth: float32 [4096, 512], P(('rows', 'sub')), may hold values from -0.25 to 0.25
Outputs:
- solved: float32 [262144, 512], P(('rows', 'sub'))
All inputs are finite; a program needn't handle non-finite values.
Results may differ from a plain program's by a relative error of at most 0.00013.
Values sent between devices are 32-bit elements; how exact they have to be, the bound alone decides.
A program may use at most 64 MiB of HBM per device.

v0:
```python
import functools

import jax
import jax.numpy as jnp
from jax import lax
from jax.experimental import pallas as pl
from jax.experimental.pallas import tpu as pltpu
from jax.sharding import PartitionSpec as P

F32 = jnp.float32
BF16 = jnp.bfloat16
MESH = pl.DeviceIdType.MESH

RANK = 256
SIDES = 512
ROWS = 1024
STREAMS = (
    (0, 512, 0, True),
    (512, 256, 1, True),
    (512, 512, 2, True),
    (0, 512, 1, True),
    (0, 512, 2, True),
    (512, 768, 3, False),
    (0, 512, 3, False),
)
G0, W1, W2, G1, G2, W3, G3 = range(7)
NS = len(STREAMS)
QUARTER = tuple(rows // 4 for _, rows, _, _ in STREAMS)
PIECE = tuple(rows // 32 for _, rows, _, _ in STREAMS)
WIDE = tuple(1 if paired else 2 for _, _, _, paired in STREAMS)
GATHERED = (W1, W2, W3)
KROWS = (8, 16, 32, 64)
KOFF = (0, 8, 24)


def split(value):
    high = value.astype(BF16)
    return high, (value - high.astype(F32)).astype(BF16)


def product(left, right, dims):
    def one(a, b):
        return lax.dot_general(a, b, (dims, ((), ())), preferred_element_type=F32)

    return one(left[0], right[0]) + (one(left[0], right[1]) + one(left[1], right[0]))


NN = ((1,), (0,))
NT = ((1,), (1,))


def solve_kernel(*refs):
    refs = list(refs)

    def take(count=None):
        if count is None:
            return refs.pop(0)
        return [refs.pop(0) for _ in range(count)]

    rhs_hbm, u_hbm, v_hbm = take(3)
    k_own = take(4)
    solved = take()
    u_in, v_in, a_hi, a_lo, v_hi, v_lo = take(6)
    part, cb, pb, rz, share, yb = [take(NS) for _ in range(6)]
    xb, xs = take(2)
    wfull = take(3)
    ffull, f_hi, f_lo, sibs, sib = take(5)
    kown, kz, k0, k1, k2, k3, kflat = take(7)
    in_sem = take()
    (core_s, core_r, pair_s, pair_r, z_s, z_r, y_s, y_r, x_s, x_r, sib_s, sib_r,
     gz_s, gz_r, gc_s, gc_r, kz_s, kz_r, kf_s, kf_r, kc_s, kc_r) = take(22)
    assert not refs

    row_index = lax.axis_index("rows")
    sub_index = lax.axis_index("sub")
    x = row_index // 16
    y = row_index // 4 % 4
    z = row_index % 4 * 2 + sub_index // 2
    c = sub_index % 2
    way = 1 - 2 * c

    def line(steps):
        return (z + way * steps + 16) % 8

    def device(x, y, z, c):
        return (x * 16 + y * 4 + z // 2, z % 2 * 2 + c)

    partner = device(x, y, z, 1 - c)
    z_peer = {steps: device(x, y, line(steps), c) for steps in (1, -1, 2, -2)}
    y_peer = [device(x, (y + d) % 4, z, c) for d in (1, 2, 3)]
    x_peer = [device((x + d) % 4, y, z, c) for d in (1, 2, 3)]
    y_odd, x_odd = y % 2, x % 2
    y_pair = device(x, y + 1 - 2 * y_odd, z, c)
    x_pair = device(x + 1 - 2 * x_odd, y, z, c)
    y_far = device(x, 3 - y, z, c)

    def describe(src, dst, s, r, to):
        return pltpu.make_async_remote_copy(
            src_ref=src, dst_ref=dst, send_sem=s, recv_sem=r, device_id=to, device_id_type=MESH
        )

    drains = {}

    def send(src, dst, s, r, to, drain):
        describe(src, dst, s, r, to).start()
        key, ref = drain
        drains[key] = (s, r, ref)

    def arrived(ref, r, s):
        describe(ref, ref, s, r, partner).wait_recv()

    barrier = pltpu.get_barrier_semaphore()
    peers = [partner] + list(z_peer.values()) + y_peer + x_peer
    for peer in peers:
        pl.semaphore_signal(barrier, inc=1, device_id=peer, device_id_type=MESH)

    loads = {}

    def load(name, src, dst, index):
        copy = pltpu.make_async_copy(src, dst, in_sem.at[index])
        copy.start()
        loads[name] = copy

    load("rhs", rhs_hbm, solved, 0)
    load("v0", v_hbm.at[0], v_in.at[0], 1)

    def load_rest():
        order = (("u", 0), ("v", 1), ("u", 1), ("v", 2), ("u", 2), ("v", 3), ("u", 3))
        for index, (name, level) in enumerate(order):
            src, dst = (u_hbm, u_in) if name == "u" else (v_hbm, v_in)
            load("%s%d" % (name, level), src.at[level], dst.at[level], 2 + index)

    kasm = (k0, k1, k2, k3)
    kline = (x_odd * 4 + y, y, y_odd, 0)

    def k_piece(which, origin):
        return kz.at[origin] if which == 0 else k3.at[0, origin, c]

    def k_send(which, index, origin, steps):
        ref = k_piece(which, origin)
        group = (0, 0, 1, 1, 2, 2, 2)[index]
        every = kz.at[0:7] if which == 0 else k3.at[0, 0:7, c]
        send(ref, ref, kz_s.at[which], kz_r.at[which, group], z_peer[steps], (("kz", which), every))

    def k_wait(which, group):
        count = (2, 2, 3)[group]
        ref = kz.at[0:count] if which == 0 else k3.at[0, 0:count, c]
        arrived(ref, kz_r.at[which, group], kz_s.at[which])

    def k_start(which):
        for level in (0, 1, 2) if which == 0 else (3,):
            count = KROWS[level] // 4
            for b in range(4):
                place = pl.ds(KOFF[level] + b if level < 3 else b, count, stride=4)
                kown[which, place, :] = k_own[level][:, b * 128:(b + 1) * 128]
        if which == 0:
            kz[z] = kown[0, 0:56, :]
        else:
            k3[0, z, c] = kown[1]
        for index, steps in enumerate((2, -2, 1, -1)):
            k_send(which, index, z, steps)

    def k_step(which):
        k_wait(which, 0)
        k_send(which, 4, line(-2), 2)
        k_send(which, 5, line(-2), 1)
        k_send(which, 6, line(2), -1)

    def k_end(which):
        k_wait(which, 1)
        k_wait(which, 2)

    def k_core(level):
        ref = kasm[level].at[:, :, c]
        send(ref, ref, kc_s.at[level], kc_r.at[level], partner, (("kc", level), ref))

    def k_lines_first():
        k_end(0)
        for level in range(3):
            kasm[level][kline[level], :, c] = kz[:, KOFF[level]:KOFF[level] + KROWS[level]]
        for d in range(3):
            send(
                kz.at[:, 0:8], k0.at[kline[0], :, c], kf_s.at[0], kf_r.at[0], y_peer[d],
                ("kf0", k0.at[0:3, :, c]),
            )

    def k_lines_more():
        for d in range(3):
            send(
                kz.at[:, 8:24], k1.at[kline[1], :, c], kf_s.at[1], kf_r.at[1], y_peer[d],
                ("kf1", k1.at[0:3, :, c]),
            )
        send(
            kz.at[:, 24:56], k2.at[kline[2], :, c], kf_s.at[2], kf_r.at[2], y_pair,
            ("kf2", k2.at[0, :, c]),
        )

    def k_far():
        arrived(k0.at[0:3, :, c], kf_r.at[0], kf_s.at[0])
        ref = k0.at[pl.ds(x_odd * 4, 4), :, c]
        send(ref, ref, kf_s.at[3], kf_r.at[3], x_pair, ("kf3", ref))

    def k_near():
        arrived(k0.at[0:4, :, c], kf_r.at[3], kf_s.at[3])
        k_core(0)

    def k_middle():
        arrived(k1.at[0:3, :, c], kf_r.at[1], kf_s.at[1])
        k_core(1)
        arrived(k2.at[0, :, c], kf_r.at[2], kf_s.at[2])
        k_core(2)

    def k_last():
        k_end(1)
        k_core(3)

    def k_matrix(level):
        arrived(kasm[level].at[:, :, c], kc_r.at[level], kc_s.at[level])
        kflat[...] = kasm[level][...].reshape(4 * RANK, 128)
        return jnp.concatenate([kflat[pl.ds(b, RANK, stride=4), :] for b in range(4)], axis=1)

    def set_a(value, first):
        turned = jnp.transpose(value)
        high, low = split(turned)
        a_hi[first:first + value.shape[1], :] = high
        a_lo[first:first + value.shape[1], :] = low

    def set_v(level):
        loads["v%d" % level].wait()
        high, low = split(v_in[level])
        v_hi[level] = high
        v_lo[level] = low

    def set_u(level):
        loads["u%d" % level].wait()
        set_a(u_in[level], 512 + RANK * level)

    def compute(s):
        if s == 0:
            loads["rhs"].wait()
            load_rest()
            set_a(solved[...], 0)
            set_v(0)
        elif s == 1:
            set_u(0)
            set_v(1)
        elif s == 2:
            set_u(1)
            set_v(2)
        elif s == 5:
            set_u(2)
            set_v(3)
        first, rows, level, _ = STREAMS[s]
        for index in range(rows // RANK):
            own = slice(first + index * RANK, first + (index + 1) * RANK)
            value = product((a_hi[own, :], a_lo[own, :]), (v_hi[level], v_lo[level]), NN)
            count = min(QUARTER[s], RANK // 4 if rows != 512 else RANK // 2)
            for at in range(0, RANK, count):
                c_at, rest = divmod(index * RANK + at, 2 * QUARTER[s])
                p_at, row = divmod(rest, QUARTER[s])
                part[s][c_at, p_at, row:row + count, :] = value[at:at + count]

    def core_send(s):
        send(part[s].at[1 - c], cb[s], core_s.at[s], core_r.at[s], partner, (("core", s), cb[s]))

    def piece(s, steps):
        lines = pl.ds(y_odd, 1) if WIDE[s] == 1 else pl.ds(0, 2)
        count = PIECE[s]
        return cb[s].at[lines, pl.ds(pl.multiple_of(line(steps) * count, count), count)]

    def z_send(s, src, index, steps):
        group = 0 if index < 3 else 1
        send(src, rz[s].at[index], z_s.at[s], z_r.at[s, group], z_peer[steps], (("z", s), rz[s]))

    def chain_first(s):
        z_send(s, piece(s, 4), 1, 2)
        z_send(s, piece(s, 3), 0, 1)
        z_send(s, piece(s, -3), 2, -1)
        z_send(s, piece(s, 1), 3, 1)
        z_send(s, piece(s, -1), 4, -1)

    def chain_second(s):
        arrived(rz[s].at[0:3], z_r.at[s, 0], z_s.at[s])
        rz[s][0] = (rz[s][0] + rz[s][1]) + piece(s, 2)[...]
        z_send(s, rz[s].at[0], 5, 2)
        rz[s][2] += piece(s, -2)[...]
        z_send(s, rz[s].at[2], 6, -2)

    def finish(s):
        arrived(rz[s].at[3:7], z_r.at[s, 1], z_s.at[s])
        share[s][...] = piece(s, 0)[...] + ((rz[s][3] + rz[s][4]) + (rz[s][5] + rz[s][6]))
        if s in (G0, W1, G1):
            to = y_peer
        elif s in (W2, G2):
            to = [y_pair]
        else:
            to = []
        for d, peer in enumerate(to):
            send(
                share[s], yb[s].at[pl.ds(d, 1)], y_s.at[s], y_r.at[s], peer,
                (("y", s), yb[s].at[0:len(to)]),
            )

    def scatter(s, stage):
        if stage == 1:
            arrived(cb[s], core_r.at[s], core_s.at[s])
            cb[s][...] += part[s][c]
            if WIDE[s] == 1:
                send(
                    cb[s].at[1 - y_odd], pb[s], pair_s.at[s], pair_r.at[s], y_pair,
                    (("pair", s), pb[s]),
                )
                return
        if WIDE[s] == 1:
            stage -= 1
            if stage == 1:
                arrived(pb[s], pair_r.at[s], pair_s.at[s])
                cb[s][y_odd] += pb[s][...]
        (None, chain_first, chain_second, finish)[stage](s)

    def by_parity(own, far):
        first = jnp.where(y_odd == 0, own, far)
        second = jnp.where(y_odd == 0, far, own)
        return jnp.concatenate([first, second], axis=0)

    def total(s):
        if s in (G0, W1, G1):
            arrived(yb[s].at[0:3], y_r.at[s], y_s.at[s])
            return by_parity(share[s][0] + yb[s][1], yb[s][0] + yb[s][2])
        if s in (W2, G2):
            arrived(yb[s].at[0:1], y_r.at[s], y_s.at[s])
            return by_parity(share[s][0], yb[s][0])
        return share[s][...].reshape(2 * PIECE[s], RANK)

    def spot(i, steps):
        full, count = (wfull[i], PIECE[GATHERED[i]]) if i < 3 else (ffull.at[i - 3], 16)
        return full.at[c, :, pl.ds(pl.multiple_of(line(steps) * count, count), count)]

    def spots(i, count):
        full, rows = (wfull[i], PIECE[GATHERED[i]]) if i < 3 else (ffull.at[i - 3], 16)
        return full.at[c, :, 0:count * rows]

    def gather_send(i, index, origin, steps):
        ref = spot(i, origin)
        group = (0, 0, 1, 1, 2, 2, 2)[index]
        send(ref, ref, gz_s.at[i], gz_r.at[i, group], z_peer[steps], (("gz", i), spots(i, 7)))

    def gather_wait(i, group):
        arrived(spots(i, (2, 2, 3)[group]), gz_r.at[i, group], gz_s.at[i])

    def gather_core(i, origin):
        ref = spot(i, origin)
        send(ref, ref, gc_s.at[i], gc_r.at[i], partner, (("gc", i), spots(i, 8)))

    def gather_put(i, value):
        spot(i, 0)[...] = value.reshape(2, value.shape[0] // 2, RANK)

    def gather_start(i):
        for index, steps in enumerate((2, -2, 1, -1)):
            gather_send(i, index, 0, steps)
        gather_core(i, 0)

    def gather_step(i):
        gather_wait(i, 0)
        gather_send(i, 4, -2, 2)
        gather_send(i, 5, -2, 1)
        gather_send(i, 6, 2, -1)
        gather_core(i, -2)
        gather_core(i, 2)
        gather_wait(i, 1)
        gather_core(i, -1)
        gather_core(i, 1)

    def gather_last(i):
        gather_wait(i, 2)
        for origin in (-4, -3, 3):
            gather_core(i, origin)

    def gather_end(i):
        arrived(spots(i, 8), gc_r.at[i], gc_s.at[i])

    def w_block(l, m):
        full = wfull[l - 1][...].reshape(l * RANK, RANK)
        return split(full[m * RANK:(m + 1) * RANK])

    factors = {}

    def pair(own, sibling, upper):
        return jnp.where(
            upper == 0,
            jnp.concatenate([own, sibling], axis=1),
            jnp.concatenate([sibling, own], axis=1),
        )

    def factor(level, paired):
        value = product(split(paired), split(k_matrix(level)), NT)
        factors[level] = split(value)
        gather_put(3 + level, value)
        if level > 0:
            gather_start(3 + level)

    def to_x():
        xs[...] = total(G0)
        for d in range(3):
            send(xs, xb.at[d], x_s.at[0], x_r.at[0], x_peer[d], ("x", xb))

    def level_0():
        arrived(xb, x_r.at[0], x_s.at[0])
        even = x_odd == 0
        own = xs[...] + jnp.where(even, xb[2], xb[0])
        sibling = xb[1] + jnp.where(even, xb[0], xb[2])
        factor(0, pair(own, sibling, x // 2))

    def level_sums(level):
        value = total((G1, G2, G3)[level - 1])
        for m in range(level):
            value = value - product(factors[m], w_block(level, m), NN)
        sibs[level - 1] = value
        to = (x_pair, y_far, y_pair)[level - 1]
        send(
            sibs.at[level - 1], sib.at[level - 1], sib_s.at[level - 1], sib_r.at[level - 1], to,
            (("sib", level), sib.at[level - 1]),
        )

    def level_factor(level):
        arrived(sib.at[level - 1], sib_r.at[level - 1], sib_s.at[level - 1])
        upper = (x_odd, y // 2, y_odd)[level - 1]
        factor(level, pair(sibs[level - 1], sib[level - 1], upper))

    block = 256
    out_copy = []

    def set_f(level):
        gather_end(3 + level)
        if level == 3:
            loads["u3"].wait()
        high, low = split(ffull[level].reshape(SIDES, RANK))
        f_hi[...] = high
        f_lo[...] = low

    def update(level):
        set_f(level)

        @pl.loop(0, ROWS // block)
        def _(i):
            rows = pl.ds(pl.multiple_of(i * block, block), block)
            solved[rows, :] -= product(split(u_in[level, rows, :]), (f_hi[...], f_lo[...]), NT)

    def w_start(i):
        gather_put(i, total(GATHERED[i]))
        gather_start(i)

    bind = functools.partial
    scatters = {}
    for s in range(NS):
        for stage in range(1, 6 - WIDE[s]):
            scatters.setdefault(s + stage, []).append(bind(scatter, s, stage))
    after = {
        2: [bind(k_step, 0)],
        3: [k_lines_first],
        5: [to_x, k_far],
        6: [bind(w_start, 0), k_near, k_lines_more, bind(k_start, 1)],
        7: [bind(gather_step, 0), bind(w_start, 1), level_0, bind(k_step, 1)],
        8: [bind(gather_step, 1), bind(gather_last, 0), bind(w_start, 2), k_middle],
        9: [
            bind(gather_end, 0), bind(level_sums, 1),
            bind(gather_step, 2), bind(gather_last, 1), bind(gather_start, 3), k_last,
            bind(level_factor, 1),
            bind(gather_end, 1), bind(level_sums, 2),
            bind(gather_last, 2), bind(gather_step, 3),
            bind(level_factor, 2),
            bind(gather_end, 2), bind(level_sums, 3),
            bind(gather_step, 4), bind(gather_last, 3),
            bind(level_factor, 3),
            bind(gather_step, 5), bind(gather_last, 4), bind(update, 0),
            bind(gather_step, 6), bind(gather_last, 5), bind(update, 1),
            bind(gather_last, 6), bind(update, 2), bind(update, 3),
        ],
    }
    for t in range(10):
        for step in scatters.get(t, []):
            step()
        for step in after.get(t, []):
            step()
        if t < NS:
            compute(t)
            if t == 0:
                pl.semaphore_wait(barrier, len(peers))
            core_send(t)
            if t == 0:
                k_start(0)
    for send_sem, recv_sem, ref in drains.values():
        describe(ref, ref, send_sem, recv_sem, partner).wait_send()


def solve(rhs, u, v, *couples):
    dma = pltpu.SemaphoreType.DMA
    any_space = pl.BlockSpec(memory_space=pl.ANY)
    pairs = []
    for sent, received in (
        ((NS,), (NS,)), ((NS,), (NS,)), ((NS,), (NS, 2)), ((NS,), (NS,)), ((1,), (1,)), ((3,), (3,)),
        ((7,), (7, 3)), ((7,), (7,)), ((2,), (2, 3)), ((4,), (4,)), ((4,), (4,)),
    ):
        pairs += [dma(sent), dma(received)]
    vm = pltpu.VMEM
    scratch = [
        vm((4, ROWS, RANK), F32), vm((4, ROWS, RANK), F32),
        vm((1280, ROWS), BF16), vm((1280, ROWS), BF16),
        vm((4, ROWS, RANK), BF16), vm((4, ROWS, RANK), BF16),
    ]
    scratch += [vm((2, 2, q, RANK), F32) for q in QUARTER]
    scratch += [vm((2, q, RANK), F32) for q in QUARTER]
    scratch += [vm((q, RANK), F32) for q in QUARTER]
    scratch += [vm((7, w, h, RANK), F32) for w, h in zip(WIDE, PIECE)]
    scratch += [vm((w, h, RANK), F32) for w, h in zip(WIDE, PIECE)]
    scratch += [vm((3, h, RANK), F32) for h in PIECE]
    scratch += [vm((3, 32, RANK), F32), vm((32, RANK), F32)]
    scratch += [vm((2, 2, QUARTER[s], RANK), F32) for s in GATHERED]
    scratch += [
        vm((4, 2, 2, 128, RANK), F32), vm((SIDES, RANK), BF16), vm((SIDES, RANK), BF16),
        vm((3, 32, RANK), F32), vm((3, 32, RANK), F32),
        vm((2, 64, 128), F32), vm((8, 56, 128), F32),
        vm((8, 8, 2, 8, 128), F32), vm((4, 8, 2, 16, 128), F32),
        vm((2, 8, 2, 32, 128), F32), vm((1, 8, 2, 64, 128), F32),
        vm((4 * RANK, 128), F32),
        dma((9,)),
    ]
    return pl.pallas_call(
        solve_kernel,
        out_shape=pltpu.VMEM((ROWS, SIDES), F32),
        in_specs=[any_space] * 3 + [pl.BlockSpec(memory_space=pltpu.VMEM)] * 4,
        out_specs=pl.BlockSpec(memory_space=pltpu.VMEM),
        scratch_shapes=scratch + pairs,
        compiler_params=pltpu.CompilerParams(
            collective_id=0, has_side_effects=True, vmem_limit_bytes=61 * 1024 * 1024
        ),
        name="solve",
    )(rhs, u, v, *couples)


def solution(mesh):
    placed = (
        P(("rows", "sub"), None),
        P(None, ("rows", "sub"), None),
        P(None, ("rows", "sub"), None),
        P(("rows", "sub"), None),
        P(("rows", "sub"), None),
        P(("rows", "sub"), None),
        P(("rows", "sub"), None),
    )
    return jax.shard_map(
        solve, mesh=mesh, in_specs=placed, out_specs=P(("rows", "sub"), None), check_vma=False
    )
```

profile of v0, /device:TPU:1, one launch (start us, length us, event | category | flops | bytes accessed | tf_op | source)
XLA Modules:
  0.0 84.7 jit_solution(5930268962339520864)
XLA Ops:
  0.0 83.3 %solve.1 = f32[1024,512]{1,0:T(8,128)S(1)} custom-call(f32[1024,512]{1,0:T(8,128)} %refs_0_.1, f32[4,1024,256]{2,1,0:T(8,128)} %refs_1_.1, f32[4,1024,256]{2,1,0:T(8,128)} %refs_2_.1, f32[2,512]{1,0:T(2,128)} %refs_3_.1, f32[4,512]{1,0:T(4,128)} %refs_4_.1, f32[8,512]{1,0:T(8,128)} %refs_5_.1, f32[16,512]{1,0:T(8,128)} %refs_6_.1), custom_call_target="tpu_custom_call" | custom-call | tf_op jit(solution)/shard_map/solve/pallas_call | solution.py:528
  83.3 1.3 %copy.9 = f32[1024,512]{1,0:T(8,128)} copy(f32[1024,512]{1,0:T(8,128)S(1)} %solve.1) | data formatting | bytes 4194304
where the time goes:
time: 84.8 us; the launch traced here: 84.7 us
  Pallas kernels  83.3 us (98%)
  local copies, waits for them, and re-layouts  1.32 us (2%)
    pallas_call x1, Pallas kernels, solve(): pl.pallas_call(solve_kernel, out_shape=pltpu.VMEM((ROWS, SIDES), F32), in...  83.3 us

commit v1 on v0

--- a/solution.py
+++ b/solution.py
@@ -15,15 +15,15 @@
 SIDES = 512
 ROWS = 1024
 STREAMS = (
-    (0, 512, 0, True),
     (512, 256, 1, True),
     (512, 512, 2, True),
+    (0, 512, 0, True),
+    (512, 768, 3, False),
     (0, 512, 1, True),
     (0, 512, 2, True),
-    (512, 768, 3, False),
     (0, 512, 3, False),
 )
-G0, W1, W2, G1, G2, W3, G3 = range(7)
+W1, W2, G0, W3, G1, G2, G3 = range(7)
 NS = len(STREAMS)
 QUARTER = tuple(rows // 4 for _, rows, _, _ in STREAMS)
 PIECE = tuple(rows // 32 for _, rows, _, _ in STREAMS)
@@ -60,7 +60,7 @@
     rhs_hbm, u_hbm, v_hbm = take(3)
     k_own = take(4)
     solved = take()
-    u_in, v_in, a_hi, a_lo, v_hi, v_lo = take(6)
+    u_in, v_in, a_hi, a_lo, v_hi, v_lo, u_hi, u_lo = take(8)
     part, cb, pb, rz, share, yb = [take(NS) for _ in range(6)]
     xb, xs = take(2)
     wfull = take(3)
@@ -121,14 +121,16 @@
         copy.start()
         loads[name] = copy
 
-    load("rhs", rhs_hbm, solved, 0)
-    load("v0", v_hbm.at[0], v_in.at[0], 1)
-
-    def load_rest():
-        order = (("u", 0), ("v", 1), ("u", 1), ("v", 2), ("u", 2), ("v", 3), ("u", 3))
-        for index, (name, level) in enumerate(order):
-            src, dst = (u_hbm, u_in) if name == "u" else (v_hbm, v_in)
-            load("%s%d" % (name, level), src.at[level], dst.at[level], 2 + index)
+    def load_group(*names):
+        for name in names:
+            index = ("u0", "v1", "u1", "v2", "rhs", "v0", "u2", "v3", "u3").index(name)
+            if name == "rhs":
+                load(name, rhs_hbm, solved, index)
+            else:
+                src, dst = (u_hbm, u_in) if name[0] == "u" else (v_hbm, v_in)
+                load(name, src.at[int(name[1])], dst.at[int(name[1])], index)
+
+    load_group("u0", "v1")
 
     kasm = (k0, k1, k2, k3)
     kline = (x_odd * 4 + y, y, y_odd, 0)
@@ -190,6 +192,8 @@
                 kz.at[:, 8:24], k1.at[kline[1], :, c], kf_s.at[1], kf_r.at[1], y_peer[d],
                 ("kf1", k1.at[0:3, :, c]),
             )
+
+    def k_lines_last():
         send(
             kz.at[:, 24:56], k2.at[kline[2], :, c], kf_s.at[2], kf_r.at[2], y_pair,
             ("kf2", k2.at[0, :, c]),
@@ -207,6 +211,8 @@
     def k_middle():
         arrived(k1.at[0:3, :, c], kf_r.at[1], kf_s.at[1])
         k_core(1)
+
+    def k_pair():
         arrived(k2.at[0, :, c], kf_r.at[2], kf_s.at[2])
         k_core(2)
 
@@ -233,21 +239,27 @@
 
     def set_u(level):
         loads["u%d" % level].wait()
-        set_a(u_in[level], 512 + RANK * level)
+        if level < 3:
+            set_a(u_in[level], 512 + RANK * level)
+        high, low = split(u_in[level])
+        u_hi[level] = high
+        u_lo[level] = low
 
     def compute(s):
-        if s == 0:
+        if s == W1:
+            set_u(0)
+            load_group("u1", "v2", "rhs")
+            set_v(1)
+        elif s == W2:
+            set_u(1)
+            load_group("v0", "u2", "v3")
+            set_v(2)
+        elif s == G0:
             loads["rhs"].wait()
-            load_rest()
+            load_group("u3")
             set_a(solved[...], 0)
             set_v(0)
-        elif s == 1:
-            set_u(0)
-            set_v(1)
-        elif s == 2:
-            set_u(1)
-            set_v(2)
-        elif s == 5:
+        elif s == W3:
             set_u(2)
             set_v(3)
         first, rows, level, _ = STREAMS[s]
@@ -379,9 +391,10 @@
     def gather_end(i):
         arrived(spots(i, 8), gc_r.at[i], gc_s.at[i])
 
-    def w_block(l, m):
-        full = wfull[l - 1][...].reshape(l * RANK, RANK)
-        return split(full[m * RANK:(m + 1) * RANK])
+    def w_block(full, l, m):
+        return split(full[l - 1][...].reshape(l * RANK, RANK)[m * RANK:(m + 1) * RANK])
+
+    sibling = (x_pair, y_far, y_pair)
 
     factors = {}
 
@@ -411,84 +424,98 @@
         sibling = xb[1] + jnp.where(even, xb[0], xb[2])
         factor(0, pair(own, sibling, x // 2))
 
+    def own_sums(level):
+        gather_end(level - 1)
+        own = sibs[level - 1]
+        for m in range(level):
+            own = own - product(factors[m], w_block(wfull, level, m), NN)
+        return own
+
+    def sums_of(level):
+        sibs[level - 1] = total((G1, G2, G3)[level - 1])
+
+    def exchange(level):
+        i = level - 1
+        send(sibs.at[i], sib.at[i], sib_s.at[i], sib_r.at[i], sibling[i], (("sib", level), sib.at[i]))
+
     def level_sums(level):
-        value = total((G1, G2, G3)[level - 1])
-        for m in range(level):
-            value = value - product(factors[m], w_block(level, m), NN)
-        sibs[level - 1] = value
-        to = (x_pair, y_far, y_pair)[level - 1]
-        send(
-            sibs.at[level - 1], sib.at[level - 1], sib_s.at[level - 1], sib_r.at[level - 1], to,
-            (("sib", level), sib.at[level - 1]),
-        )
+        sibs[level - 1] = own_sums(level)
+        exchange(level)
 
     def level_factor(level):
-        arrived(sib.at[level - 1], sib_r.at[level - 1], sib_s.at[level - 1])
-        upper = (x_odd, y // 2, y_odd)[level - 1]
-        factor(level, pair(sibs[level - 1], sib[level - 1], upper))
+        i = level - 1
+        arrived(sib.at[i], sib_r.at[i], sib_s.at[i])
+        factor(level, pair(sibs[i], sib[i], (x_odd, y // 2, y_odd)[i]))
 
     block = 256
-    out_copy = []
-
-    def set_f(level):
+
+    def update(level):
         gather_end(3 + level)
-        if level == 3:
-            loads["u3"].wait()
         high, low = split(ffull[level].reshape(SIDES, RANK))
         f_hi[...] = high
         f_lo[...] = low
-
-    def update(level):
-        set_f(level)
-
-        @pl.loop(0, ROWS // block)
-        def _(i):
-            rows = pl.ds(pl.multiple_of(i * block, block), block)
-            solved[rows, :] -= product(split(u_in[level, rows, :]), (f_hi[...], f_lo[...]), NT)
+        for i in range(ROWS // block):
+            rows = pl.ds(i * block, block)
+            solved[rows, :] -= product(
+                (u_hi[level, rows, :], u_lo[level, rows, :]), (f_hi[...], f_lo[...]), NT
+            )
+
+    def update_half(near):
+        core = c if near else 1 - c
+        if not near:
+            gather_end(6)
+        high, low = split(ffull[3, core].reshape(RANK, RANK))
+        place = slice(0, RANK) if near else slice(RANK, SIDES)
+        f_hi[place, :] = high
+        f_lo[place, :] = low
+        columns = pl.ds(pl.multiple_of(core * RANK, RANK), RANK)
+        for i in range(ROWS // block):
+            rows = pl.ds(i * block, block)
+            solved[rows, columns] -= product(
+                (u_hi[3, rows, :], u_lo[3, rows, :]), (f_hi[place, :], f_lo[place, :]), NT
+            )
 
     def w_start(i):
         gather_put(i, total(GATHERED[i]))
         gather_start(i)
 
     bind = functools.partial
-    scatters = {}
-    for s in range(NS):
-        for stage in range(1, 6 - WIDE[s]):
-            scatters.setdefault(s + stage, []).append(bind(scatter, s, stage))
-    after = {
-        2: [bind(k_step, 0)],
-        3: [k_lines_first],
-        5: [to_x, k_far],
-        6: [bind(w_start, 0), k_near, k_lines_more, bind(k_start, 1)],
-        7: [bind(gather_step, 0), bind(w_start, 1), level_0, bind(k_step, 1)],
-        8: [bind(gather_step, 1), bind(gather_last, 0), bind(w_start, 2), k_middle],
-        9: [
-            bind(gather_end, 0), bind(level_sums, 1),
-            bind(gather_step, 2), bind(gather_last, 1), bind(gather_start, 3), k_last,
-            bind(level_factor, 1),
-            bind(gather_end, 1), bind(level_sums, 2),
-            bind(gather_last, 2), bind(gather_step, 3),
-            bind(level_factor, 2),
-            bind(gather_end, 2), bind(level_sums, 3),
-            bind(gather_step, 4), bind(gather_last, 3),
-            bind(level_factor, 3),
-            bind(gather_step, 5), bind(gather_last, 4), bind(update, 0),
-            bind(gather_step, 6), bind(gather_last, 5), bind(update, 1),
-            bind(gather_last, 6), bind(update, 2), bind(update, 3),
-        ],
-    }
-    for t in range(10):
-        for step in scatters.get(t, []):
-            step()
-        for step in after.get(t, []):
-            step()
-        if t < NS:
-            compute(t)
-            if t == 0:
-                pl.semaphore_wait(barrier, len(peers))
-            core_send(t)
-            if t == 0:
-                k_start(0)
+    def make(s):
+        compute(s)
+        core_send(s)
+
+    def sc(s, stage):
+        return bind(scatter, s, stage)
+
+    def enter():
+        pl.semaphore_wait(barrier, len(peers))
+        core_send(W1)
+        core_send(W2)
+        k_start(0)
+
+    order = [
+        bind(compute, W1), bind(compute, W2), enter, bind(k_start, 1),
+        sc(W1, 1), bind(make, G0), sc(W2, 1),
+        bind(make, W3), sc(W1, 2), bind(k_step, 0), sc(G0, 1), sc(W3, 1),
+        bind(make, G1), sc(W2, 2), bind(make, G2), bind(k_step, 1), sc(G1, 1), sc(W1, 3),
+        bind(make, G3), k_lines_first, sc(G0, 2), sc(G2, 1), sc(W2, 3), sc(W1, 4),
+        sc(W3, 2), sc(G3, 1), sc(G1, 2), sc(G0, 3), k_far, k_last, sc(W2, 4), bind(w_start, 0),
+        sc(G2, 2), sc(G0, 4), sc(G1, 3), k_lines_more, bind(set_u, 3),
+        bind(w_start, 1), bind(gather_step, 0), sc(W3, 3), to_x, sc(G2, 3), sc(G1, 4),
+        bind(w_start, 2), k_near,
+        bind(gather_last, 0), bind(gather_step, 1), sc(G2, 4), bind(sums_of, 1), k_lines_last,
+        level_0, bind(gather_step, 2), sc(G3, 2), bind(level_sums, 1),
+        bind(gather_last, 1), k_middle, bind(sums_of, 2), bind(gather_last, 2),
+        bind(level_factor, 1), k_pair, bind(level_sums, 2), sc(G3, 3), bind(gather_start, 3),
+        bind(level_factor, 2), bind(sums_of, 3), bind(level_sums, 3),
+        bind(gather_step, 4), bind(gather_step, 3), bind(level_factor, 3),
+        bind(gather_step, 5), bind(gather_last, 4), bind(gather_last, 3),
+        bind(gather_step, 6), bind(update, 1), bind(update, 0),
+        bind(gather_last, 5), bind(gather_last, 6), bind(update, 2),
+        bind(update_half, True), bind(update_half, False),
+    ]
+    for step in order:
+        step()
     for send_sem, recv_sem, ref in drains.values():
         describe(ref, ref, send_sem, recv_sem, partner).wait_send()
 
@@ -506,6 +533,7 @@
     scratch = [
         vm((4, ROWS, RANK), F32), vm((4, ROWS, RANK), F32),
         vm((1280, ROWS), BF16), vm((1280, ROWS), BF16),
+        vm((4, ROWS, RANK), BF16), vm((4, ROWS, RANK), BF16),
         vm((4, ROWS, RANK), BF16), vm((4, ROWS, RANK), BF16),
     ]
     scratch += [vm((2, 2, q, RANK), F32) for q in QUARTER]

time: 84.8 us -> 73.5 us (0.87)
  Pallas kernels: 83.3 us -> 72 us
    pallas_call x1, Pallas kernels: 83.3 us -> 72 us  [solve(): pl.pallas_call(solve_kernel, out_shape=pltpu.VMEM((ROWS, SIDES), F32), in...]
where the time goes in v1:
time: 73.5 us; the launch traced here: 73.3 us
  Pallas kernels  72 us (98%)
  local copies, waits for them, and re-layouts  1.32 us (2%)
    pallas_call x1, Pallas kernels, solve(): pl.pallas_call(solve_kernel, out_shape=pltpu.VMEM((ROWS, SIDES), F32), in...  72 us

profile of v1, /device:TPU:1, one launch (start us, length us, event | category | flops | bytes accessed | tf_op | source)
XLA Modules:
  0.0 73.3 jit_solution(8280105039921381265)
XLA Ops:
  0.0 72.0 %solve.1 = f32[1024,512]{1,0:T(8,128)S(1)} custom-call(f32[1024,512]{1,0:T(8,128)} %refs_0_.1, f32[4,1024,256]{2,1,0:T(8,128)} %refs_1_.1, f32[4,1024,256]{2,1,0:T(8,128)} %refs_2_.1, f32[2,512]{1,0:T(2,128)} %refs_3_.1, f32[4,512]{1,0:T(4,128)} %refs_4_.1, f32[8,512]{1,0:T(8,128)} %refs_5_.1, f32[16,512]{1,0:T(8,128)} %refs_6_.1), custom_call_target="tpu_custom_call" | custom-call | tf_op jit(solution)/shard_map/solve/pallas_call | solution.py:556
  72.0 1.3 %copy.9 = f32[1024,512]{1,0:T(8,128)} copy(f32[1024,512]{1,0:T(8,128)S(1)} %solve.1) | data formatting | bytes 4194304

commit v2 on v1

--- a/solution.py
+++ b/solution.py
@@ -298,9 +298,26 @@
         rz[s][2] += piece(s, -2)[...]
         z_send(s, rz[s].at[2], 6, -2)
 
+    def long_chain(s, k):
+        if k > 1:
+            arrived(rz[s].at[0:2], z_r.at[s, k - 2], z_s.at[s])
+            rz[s][k - 2] += piece(s, 5 - k)[...]
+        if 1 < k <= 3:
+            rz[s][k + 2] += piece(s, k - 4)[...]
+        drain = (("z", s), rz[s])
+        up = piece(s, 4) if k == 1 else rz[s].at[k - 2]
+        send(up, rz[s].at[k - 1], z_s.at[s], z_r.at[s, k - 1], z_peer[1], drain)
+        if k <= 3:
+            down = piece(s, -3) if k == 1 else rz[s].at[k + 2]
+            send(down, rz[s].at[k + 3], z_s.at[s], z_r.at[s, k - 1], z_peer[-1], drain)
+
     def finish(s):
-        arrived(rz[s].at[3:7], z_r.at[s, 1], z_s.at[s])
-        share[s][...] = piece(s, 0)[...] + ((rz[s][3] + rz[s][4]) + (rz[s][5] + rz[s][6]))
+        if WIDE[s] == 1:
+            arrived(rz[s].at[3:7], z_r.at[s, 1], z_s.at[s])
+            share[s][...] = piece(s, 0)[...] + ((rz[s][3] + rz[s][4]) + (rz[s][5] + rz[s][6]))
+        else:
+            arrived(rz[s].at[0:1], z_r.at[s, 3], z_s.at[s])
+            share[s][...] = piece(s, 0)[...] + (rz[s][3] + rz[s][6])
         if s in (G0, W1, G1):
             to = y_peer
         elif s in (W2, G2):
@@ -328,7 +345,11 @@
             if stage == 1:
                 arrived(pb[s], pair_r.at[s], pair_s.at[s])
                 cb[s][y_odd] += pb[s][...]
-        (None, chain_first, chain_second, finish)[stage](s)
+            (None, chain_first, chain_second, finish)[stage](s)
+        elif stage <= 4:
+            long_chain(s, stage)
+        else:
+            finish(s)
 
     def by_parity(own, far):
         first = jnp.where(y_odd == 0, own, far)
@@ -498,20 +519,19 @@
         sc(W1, 1), bind(make, G0), sc(W2, 1),
         bind(make, W3), sc(W1, 2), bind(k_step, 0), sc(G0, 1), sc(W3, 1),
         bind(make, G1), sc(W2, 2), bind(make, G2), bind(k_step, 1), sc(G1, 1), sc(W1, 3),
-        bind(make, G3), k_lines_first, sc(G0, 2), sc(G2, 1), sc(W2, 3), sc(W1, 4),
-        sc(W3, 2), sc(G3, 1), sc(G1, 2), sc(G0, 3), k_far, k_last, sc(W2, 4), bind(w_start, 0),
-        sc(G2, 2), sc(G0, 4), sc(G1, 3), k_lines_more, bind(set_u, 3),
-        bind(w_start, 1), bind(gather_step, 0), sc(W3, 3), to_x, sc(G2, 3), sc(G1, 4),
-        bind(w_start, 2), k_near,
-        bind(gather_last, 0), bind(gather_step, 1), sc(G2, 4), bind(sums_of, 1), k_lines_last,
-        level_0, bind(gather_step, 2), sc(G3, 2), bind(level_sums, 1),
-        bind(gather_last, 1), k_middle, bind(sums_of, 2), bind(gather_last, 2),
-        bind(level_factor, 1), k_pair, bind(level_sums, 2), sc(G3, 3), bind(gather_start, 3),
-        bind(level_factor, 2), bind(sums_of, 3), bind(level_sums, 3),
-        bind(gather_step, 4), bind(gather_step, 3), bind(level_factor, 3),
-        bind(gather_step, 5), bind(gather_last, 4), bind(gather_last, 3),
-        bind(gather_step, 6), bind(update, 1), bind(update, 0),
-        bind(gather_last, 5), bind(gather_last, 6), bind(update, 2),
+        bind(make, G3), sc(W3, 2), k_lines_first, sc(G0, 2), sc(G2, 1), sc(W2, 3), sc(W1, 4),
+        sc(W3, 3), sc(G0, 3), sc(G1, 2), sc(G3, 1), k_far, k_last, sc(W2, 4), bind(w_start, 0),
+        sc(W3, 4), sc(G2, 2), sc(G0, 4), sc(G1, 3), bind(w_start, 1), bind(set_u, 3), sc(G3, 2),
+        bind(gather_step, 0), sc(W3, 5), bind(w_start, 2), to_x, sc(G2, 3), sc(G1, 4), sc(G3, 3),
+        k_lines_more, bind(gather_last, 0), bind(gather_step, 1), sc(G2, 4), bind(sums_of, 1),
+        k_lines_last, k_near, sc(G3, 4),
+        level_0, bind(level_sums, 1), bind(gather_step, 2), bind(gather_start, 3), k_middle,
+        bind(gather_last, 1), bind(sums_of, 2), sc(G3, 5),
+        bind(level_factor, 1), k_pair, bind(level_sums, 2), bind(gather_last, 2),
+        bind(gather_step, 3), bind(level_factor, 2), bind(sums_of, 3), bind(level_sums, 3),
+        bind(gather_step, 4), bind(gather_last, 3), bind(level_factor, 3),
+        bind(gather_step, 5), bind(update, 0), bind(gather_last, 4), bind(gather_step, 6),
+        bind(update, 1), bind(gather_last, 5), bind(gather_last, 6), bind(update, 2),
         bind(update_half, True), bind(update_half, False),
     ]
     for step in order:
@@ -525,7 +545,7 @@
     any_space = pl.BlockSpec(memory_space=pl.ANY)
     pairs = []
     for sent, received in (
-        ((NS,), (NS,)), ((NS,), (NS,)), ((NS,), (NS, 2)), ((NS,), (NS,)), ((1,), (1,)), ((3,), (3,)),
+        ((NS,), (NS,)), ((NS,), (NS,)), ((NS,), (NS, 4)), ((NS,), (NS,)), ((1,), (1,)), ((3,), (3,)),
         ((7,), (7, 3)), ((7,), (7,)), ((2,), (2, 3)), ((4,), (4,)), ((4,), (4,)),
     ):
         pairs += [dma(sent), dma(received)]

time: 73.5 us -> 71.6 us (0.974)
  Pallas kernels: 72 us -> 70.1 us
    pallas_call x1, Pallas kernels: 72 us -> 70.1 us  [solve(): pl.pallas_call(solve_kernel, out_shape=pltpu.VMEM((ROWS, SIDES), F32), in...]
where the time goes in v2:
time: 71.6 us; the launch traced here: 71.5 us
  Pallas kernels  70.1 us (98%)
  local copies, waits for them, and re-layouts  1.32 us (2%)
    pallas_call x1, Pallas kernels, solve(): pl.pallas_call(solve_kernel, out_shape=pltpu.VMEM((ROWS, SIDES), F32), in...  70.1 us

profile of v2, /device:TPU:1, one launch (start us, length us, event | category | flops | bytes accessed | tf_op | source)
XLA Modules:
  0.0 71.5 jit_solution(3549631857023788618)
XLA Ops:
  0.0 70.1 %solve.1 = f32[1024,512]{1,0:T(8,128)S(1)} custom-call(f32[1024,512]{1,0:T(8,128)} %refs_0_.1, f32[4,1024,256]{2,1,0:T(8,128)} %refs_1_.1, f32[4,1024,256]{2,1,0:T(8,128)} %refs_2_.1, f32[2,512]{1,0:T(2,128)} %refs_3_.1, f32[4,512]{1,0:T(4,128)} %refs_4_.1, f32[8,512]{1,0:T(8,128)} %refs_5_.1, f32[16,512]{1,0:T(8,128)} %refs_6_.1), custom_call_target="tpu_custom_call" | custom-call | tf_op jit(solution)/shard_map/solve/pallas_call | solution.py:576
  70.1 1.3 %copy.9 = f32[1024,512]{1,0:T(8,128)} copy(f32[1024,512]{1,0:T(8,128)S(1)} %solve.1) | data formatting | bytes 4194304

commit v3 on v2

--- a/solution.py
+++ b/solution.py
@@ -521,11 +521,11 @@
         bind(make, G1), sc(W2, 2), bind(make, G2), bind(k_step, 1), sc(G1, 1), sc(W1, 3),
         bind(make, G3), sc(W3, 2), k_lines_first, sc(G0, 2), sc(G2, 1), sc(W2, 3), sc(W1, 4),
         sc(W3, 3), sc(G0, 3), sc(G1, 2), sc(G3, 1), k_far, k_last, sc(W2, 4), bind(w_start, 0),
-        sc(W3, 4), sc(G2, 2), sc(G0, 4), sc(G1, 3), bind(w_start, 1), bind(set_u, 3), sc(G3, 2),
+        sc(W3, 4), sc(G2, 2), sc(G0, 4), sc(G1, 3), bind(w_start, 1), bind(set_u, 3), sc(G3, 2), k_near,
         bind(gather_step, 0), sc(W3, 5), bind(w_start, 2), to_x, sc(G2, 3), sc(G1, 4), sc(G3, 3),
-        k_lines_more, bind(gather_last, 0), bind(gather_step, 1), sc(G2, 4), bind(sums_of, 1),
-        k_lines_last, k_near, sc(G3, 4),
-        level_0, bind(level_sums, 1), bind(gather_step, 2), bind(gather_start, 3), k_middle,
+        k_lines_more, bind(gather_last, 0), bind(gather_step, 1), bind(sums_of, 1),
+        k_lines_last, level_0, bind(level_sums, 1), sc(G2, 4), sc(G3, 4),
+        bind(gather_step, 2), bind(gather_start, 3), k_middle,
         bind(gather_last, 1), bind(sums_of, 2), sc(G3, 5),
         bind(level_factor, 1), k_pair, bind(level_sums, 2), bind(gather_last, 2),
         bind(gather_step, 3), bind(level_factor, 2), bind(sums_of, 3), bind(level_sums, 3),

time: 71.6 us -> 70 us (0.978)
  Pallas kernels: 70.1 us -> 68.5 us
    pallas_call x1, Pallas kernels: 70.1 us -> 68.5 us  [solve(): pl.pallas_call(solve_kernel, out_shape=pltpu.VMEM((ROWS, SIDES), F32), in...]
where the time goes in v3:
time: 70 us; the launch traced here: 69.9 us
  Pallas kernels  68.5 us (98%)
  local copies, waits for them, and re-layouts  1.32 us (2%)
    pallas_call x1, Pallas kernels, solve(): pl.pallas_call(solve_kernel, out_shape=pltpu.VMEM((ROWS, SIDES), F32), in...  68.5 us

profile of v3, /device:TPU:1, one launch (start us, length us, event | category | flops | bytes accessed | tf_op | source)
XLA Modules:
  0.0 69.9 jit_solution(8259954444827784001)
XLA Ops:
  0.0 68.5 %solve.1 = f32[1024,512]{1,0:T(8,128)S(1)} custom-call(f32[1024,512]{1,0:T(8,128)} %refs_0_.1, f32[4,1024,256]{2,1,0:T(8,128)} %refs_1_.1, f32[4,1024,256]{2,1,0:T(8,128)} %refs_2_.1, f32[2,512]{1,0:T(2,128)} %refs_3_.1, f32[4,512]{1,0:T(4,128)} %refs_4_.1, f32[8,512]{1,0:T(8,128)} %refs_5_.1, f32[16,512]{1,0:T(8,128)} %refs_6_.1), custom_call_target="tpu_custom_call" | custom-call | tf_op jit(solution)/shard_map/solve/pallas_call | solution.py:576
  68.6 1.3 %copy.9 = f32[1024,512]{1,0:T(8,128)} copy(f32[1024,512]{1,0:T(8,128)S(1)} %solve.1) | data formatting | bytes 4194304
